TPU v7x, 32 devices: a whole 2x2x4 slice. The times are simulated.
32 devices in a mesh: grid: 4 (over z), orb: 4 (over y, core), pts: 2 (over x).
Axes of the slice: x: 2, y: 2, z: 4, core: 2. Of those that a mesh axis runs over, the one named last changes fastest.
Arguments:
- orbitals: bfloat16 [1024, 2048], P('grid', 'orb'), may hold values from -6 to 6
- points: int32 [8192], replicated, may hold values from 0 to 1023
- fitting: bfloat16 [1024, 8192], P('grid', ('orb', 'pts')), may hold values from -0.0625 to 0.0625
- screened: bfloat16 [8192, 8192], P(('orb', 'pts'), 'grid'), may hold values from -0.0014648438 to 0.0014648438
Outputs:
- exchange_orbitals: float32 [2048, 1024], P(('orb', 'pts'), 'grid')
- exchange_matrix: float32 [2048, 2048], P(('orb', 'pts'), 'grid')
Inputs may be any that keep to these rules, and one draw needn't show every extreme that they name: Grid rows of the window; two points may name the same row.
All inputs are finite; a program needn't handle non-finite values.
Results may differ from a plain program's by a relative error of at most 0.005.
Values may be sent and summed in bfloat16 or wider, within the bound.
A program may use at most 128 MiB of HBM per device.

v0:
```python
import math
import jax
import jax.numpy as jnp
from jax import lax
from jax.sharding import PartitionSpec as P


def per_device(orbitals, points, fitting, screened):
    grid_index = lax.axis_index("grid")
    orb_index = lax.axis_index("orb")
    pts_index = lax.axis_index("pts")
    n_grid = lax.axis_size("grid")
    n_orb = lax.axis_size("orb")
    n_pts = lax.axis_size("pts")
    rows_dev, width_dev = orbitals.shape
    npoints = points.shape[0]
    point_block = npoints // (n_orb * n_pts)
    column_block = npoints // n_grid
    local_rows = points - grid_index * rows_dev
    inside = (local_rows >= 0) & (local_rows < rows_dev)
    clamped = jnp.clip(local_rows, 0, rows_dev - 1)
    taken = jnp.take(orbitals, clamped, axis=0).astype(jnp.float32)
    selected = jnp.where(inside[:, None], taken, jnp.zeros_like(taken))
    picked = lax.psum(selected.astype(jnp.bfloat16), "grid")
    grouped = picked.reshape(n_orb, n_pts, point_block, width_dev)
    own_rows = lax.dynamic_index_in_dim(grouped, pts_index, 1, keepdims=False).reshape(
        n_orb * point_block, width_dev
    )
    point_rows = lax.dynamic_slice_in_dim(picked, grid_index * column_block, column_block, 0)
    rows_full, point_full = (
        lax.all_gather(own_rows, "orb", axis=1, tiled=True),
        lax.all_gather(point_rows, "orb", axis=1, tiled=True),
    )
    own_full = lax.dynamic_slice_in_dim(rows_full, orb_index * point_block, point_block, 0)
    density = lax.dot_general(
        own_full, point_full, (((1,), (1,)), ((), ())), preferred_element_type=jnp.float32
    )
    masked = (density * screened.astype(jnp.float32)).astype(jnp.bfloat16)
    partial_applied = jnp.dot(masked, point_full, preferred_element_type=jnp.float32)
    applied = lax.psum(partial_applied, "grid").astype(jnp.bfloat16)
    terms = lax.psum_scatter(
        -lax.dot_general(
            applied, fitting, (((0,), (1,)), ((), ())), preferred_element_type=jnp.float32
        ),
        ("orb", "pts"),
        scatter_dimension=0,
        tiled=True,
    )
    rounded = terms.astype(jnp.bfloat16)
    partial_matrix = jnp.dot(
        rounded,
        lax.all_gather(orbitals, "orb", axis=1, tiled=True),
        preferred_element_type=jnp.float32,
    )
    summed = lax.psum_scatter(partial_matrix, "grid", scatter_dimension=1, tiled=True)
    exchange_matrix = summed / math.sqrt(rows_dev * n_grid)
    return (terms, exchange_matrix)


def solution(mesh):
    in_specs = (P("grid", "orb"), P(), P("grid", ("orb", "pts")), P(("orb", "pts"), "grid"))
    out_specs = (P(("orb", "pts"), "grid"), P(("orb", "pts"), "grid"))
    return jax.shard_map(
        per_device, mesh=mesh, in_specs=in_specs, out_specs=out_specs, check_vma=False
    )
```

profile of v0, /device:TPU:0, one launch (start us, length us, event | category | flops | bytes accessed | tf_op | source)
XLA Modules:
  0.0 927.6 jit_solution(6591598182595387034)
XLA Ops:
  7.2 0.0 copy-start
  7.2 0.0 all-reduce.3.cloned.1.call-start
  7.2 0.8 compare_and_fusion.1
  8.1 0.8 fusion.11
  8.8 34.9 %gather_fusion = bf16[8192,512]{1,0:T(8,128)(2,1)} fusion(bf16[256,512]{1,0:T(8,128)(2,1)} %param.4, s32[8192]{0:T(1024)S(1)} %fusion.11), kind=kCustom, calls=%fused_computation | custom fusion | bytes 16809984 | tf_op jit(solution)/shard_map/jit(_take)/gather | solution.py:22
  43.8 8.5 select_convert_fusion
  52.3 0.0 all-reduce.3.cloned.1.call-update
  52.3 0.0 all-gather.6.cloned.1.call-start
  52.4 293.7 %all-reduce.3.cloned.1.call-done = bf16[8192,512]{1,0:T(8,128)(2,1)} async-done(((bf16[8192,512]{1,0:T(8,128)(2,1)}), bf16[8192,512]{1,0:T(8,128)(2,1)}) %all-reduce.3.cloned.1.call-update) | async-done | bytes 8388624 | tf_op jit(solution)/shard_map/psum | solution.py:24
  346.0 3.0 constant_dynamic-slice_fusion
  349.1 0.0 all-gather.6.cloned.1.call-update
  349.1 0.0 all-gather.4.cloned.1.call-start
  349.2 4.4 constant_dynamic-slice_fusion.1
  353.6 0.0 all-gather.4.cloned.1.call-update
  353.6 0.0 all-gather.8.cloned.1.call-start
  353.7 0.5 all-gather.8.cloned.1.call-update
  354.2 0.0 reduce-scatter.3.cloned.1.call-start
  354.2 52.3 %all-gather.6.cloned.1.call-done = bf16[2048,2048]{1,0:T(8,128)(2,1)} async-done(((bf16[2048,512]{1,0:T(8,128)(2,1)}), bf16[2048,2048]{1,0:T(8,128)(2,1)}) %all-gather.6.cloned.1.call-update) | async-done | bytes 8388624 | tf_op jit(solution)/shard_map/all_gather | solution.py:32
  406.5 107.5 %all-gather.4.cloned.1.call-done = bf16[4096,2048]{1,0:T(8,128)(2,1)} async-done(((bf16[4096,512]{1,0:T(8,128)(2,1)}), bf16[4096,2048]{1,0:T(8,128)(2,1)}) %all-gather.4.cloned.1.call-update) | async-done | bytes 16777232 | tf_op jit(solution)/shard_map/all_gather | solution.py:31
  514.0 27.6 %fusion.4 = f32[1024,2048]{1,0:T(8,128)} fusion(bf16[2048,2048]{1,0:T(8,128)(2,1)} %all-gather.6.cloned.1.call-done, bf16[1024,2048]{1,0:T(8,128)(2,1)} %param.7, bf16[4096,2048]{1,0:T(8,128)(2,1)} %all-gather.4.cloned.1.call-done, s32[]{:T(128)S(6)} %select_n.27), kind=kOutput, calls=%fused_computation.6 | convolution fusion | flops 17186160640 | bytes 33554436 | tf_op jit(solution)/shard_map/dot_general | solution.py:39
  541.6 286.5 %all-reduce.4 = bf16[1024,2048]{1,0:T(8,128)(2,1)} all-reduce(f32[1024,2048]{1,0:T(8,128)} %fusion.4), channel_id=1, replica_groups=mesh['grid'=4,'orb'=4,'pts'=2] {'grid'}, use_global_device_ids=true, to_apply=%region_1.2 | all-reduce | flops 2097152 | bytes 12582912 | tf_op jit(solution)/shard_map/psum | solution.py:40
  828.1 0.0 copy-done
  828.1 4.8 fusion.6
  833.0 0.0 reduce-scatter.3.cloned.1.call-update
  833.0 0.0 reduce-scatter.5.cloned.1.call-start
  833.0 0.0 all-gather.8.cloned.1.call-done
  833.1 38.9 %reduce-scatter.3.cloned.1.call-done = f32[256,256]{1,0:T(8,128)} async-done(((f32[2048,256]{1,0:T(8,128)}), f32[256,256]{1,0:T(8,128)}) %reduce-scatter.3.cloned.1.call-update) | async-done | bytes 262160 | tf_op jit(solution)/shard_map/reduce_scatter | solution.py:41
  872.0 3.1 fusion.9
  875.1 0.0 reduce-scatter.5.cloned.1.call-update
  875.1 43.8 %reduce-scatter.5.cloned.1.call-done = f32[256,512]{1,0:T(8,128)} async-done(((f32[256,2048]{1,0:T(8,128)}), f32[256,512]{1,0:T(8,128)}) %reduce-scatter.5.cloned.1.call-update) | async-done | bytes 524304 | tf_op jit(solution)/shard_map/reduce_scatter | solution.py:55
  918.9 1.9 broadcast_multiply_fusion
Async XLA Ops:
  7.2 821.0 %copy-start = (bf16[256,1024]{1,0:T(8,128)(2,1)S(1)}, bf16[256,1024]{1,0:T(8,128)(2,1)}, u32[]{:S(2)}) copy-start(bf16[256,1024]{1,0:T(8,128)(2,1)} %param.6) | copy-start | bytes 1572868
  7.2 338.9 %all-reduce.3.cloned.1.call-start = ((), (), s32[]{:S(2)}) async-start(), calls=%async_computation.2 | async-start | bytes 16777216 | tf_op jit(solution)/shard_map/psum | solution.py:24
  52.3 354.2 %all-gather.6.cloned.1.call-start = ((), (), s32[]{:S(2)}) async-start(), calls=%async_computation.4 | async-start | bytes 10485760 | tf_op jit(solution)/shard_map/all_gather | solution.py:32
  349.1 164.9 %all-gather.4.cloned.1.call-start = ((), (), s32[]{:S(2)}) async-start(), calls=%async_computation.3 | async-start | bytes 20971520 | tf_op jit(solution)/shard_map/all_gather | solution.py:31
  353.6 479.4 %all-gather.8.cloned.1.call-start = ((), (), s32[]{:S(2)}) async-start(), calls=%async_computation.6 | async-start | bytes 1310720 | tf_op jit(solution)/shard_map/all_gather | solution.py:52
  354.2 517.8 %reduce-scatter.3.cloned.1.call-start = ((), (), s32[]{:S(2)}) async-start(), calls=%async_computation.5 | async-start | bytes 2359296 | tf_op jit(solution)/shard_map/reduce_scatter | solution.py:41
  833.0 85.9 %reduce-scatter.5.cloned.1.call-start = ((), (), s32[]{:S(2)}) async-start(), calls=%async_computation.7 | async-start | bytes 2621440 | tf_op jit(solution)/shard_map/reduce_scatter | solution.py:55
Sparse Core Ops, SparseCore 0:
  52.5 293.5 all-reduce.2
  349.2 57.2 all-gather.5
  408.1 105.8 all-gather.3
  515.4 16.6 all-gather.7
  833.1 38.8 reduce-scatter.2
  875.2 43.5 reduce-scatter.4
where the time goes:
time: 928 us
  waiting for transfers between devices  537 us (58%)
  blocking collectives  287 us (31%)
  local copies, waits for them, and re-layouts  42.4 us (5%)
  matrix products  35.5 us (4%)
  between operations  14.2 us (2%)
  other arithmetic  12 us (1%)
    psum x1, waiting for transfers between devices, per_device(): picked = lax.psum(selected.astype(jnp.bfloat16), 'grid')  294 us
    psum x1, blocking collectives, per_device(): applied = lax.psum(partial_applied, 'grid').astype(jnp.bfloat16)  287 us
    all_gather x1, waiting for transfers between devices, per_device(): lax.all_gather(own_rows, 'orb', axis=1, tiled=True)  107 us
    all_gather x1, waiting for transfers between devices, per_device(): lax.all_gather(point_rows, 'orb', axis=1, tiled=True)  52.3 us
    reduce_scatter x1, waiting for transfers between devices, per_device(): lax.psum_scatter(partial_matrix, 'grid', scatter_dimension=1, tiled=True)  43.8 us
    reduce_scatter x1, waiting for transfers between devices, per_device(): lax.psum_scatter(-lax.dot_general(applied, fitting, (((0,), (1,)), ((), (...  38.9 us
    gather x1, local copies, waits for them, and re-layouts, per_device(): taken = jnp.take(orbitals, clamped, axis=0).astype(jnp.float32)  34.9 us
    dot_general x1, matrix products, per_device(): jnp.dot(masked, point_full, preferred_element_type=jnp.float32)  27.6 us
  transfers between devices with their start and end apart: 6, of which 5 were waited for; matrix products, arithmetic and copies ran while one was open for 4% of the time, Pallas kernels for 0%

commit v1 on v0

--- a/solution.py
+++ b/solution.py
@@ -21,7 +21,7 @@
     clamped = jnp.clip(local_rows, 0, rows_dev - 1)
     taken = jnp.take(orbitals, clamped, axis=0).astype(jnp.float32)
     selected = jnp.where(inside[:, None], taken, jnp.zeros_like(taken))
-    picked = lax.psum(selected.astype(jnp.bfloat16), "grid")
+    picked = jnp.sum(lax.all_gather(selected.astype(jnp.bfloat16), "grid"), axis=0)
     grouped = picked.reshape(n_orb, n_pts, point_block, width_dev)
     own_rows = lax.dynamic_index_in_dim(grouped, pts_index, 1, keepdims=False).reshape(
         n_orb * point_block, width_dev

time: 928 us -> 1220 us (1.31)
  waiting for transfers between devices: 537 us -> 807 us
  other arithmetic: 12 us -> 28.4 us
    all_gather x0 -> x1, waiting for transfers between devices: none -> 564 us  [per_device(): lax.all_gather(selected.astype(jnp.bfloat16), 'grid')]
    psum x1 -> x0, waiting for transfers between devices: 294 us -> none  [per_device(): picked = lax.psum(selected.astype(jnp.bfloat16), 'grid')]
    reduce_sum x0 -> x1, other arithmetic: none -> 16.3 us  [per_device(): jnp.sum(lax.all_gather(selected.astype(jnp.bfloat16), 'grid'), axis=0)]
  transfers between devices with their start and end apart: 6 -> 6, of which waited for: 5 -> 5; matrix products, arithmetic and copies ran while one was open for 4% -> 3% of each run, Pallas kernels for 0% -> 0%
where the time goes in v1:
time: 1220 us; the launch traced here: 1210 us
  waiting for transfers between devices  807 us (66%)
  blocking collectives  287 us (24%)
  local copies, waits for them, and re-layouts  42.4 us (3%)
  matrix products  35.6 us (3%)
  other arithmetic  28.4 us (2%)
  between operations  14.1 us (1%)
    all_gather x1, waiting for transfers between devices, per_device(): lax.all_gather(selected.astype(jnp.bfloat16), 'grid')  564 us
    psum x1, blocking collectives, per_device(): applied = lax.psum(partial_applied, 'grid').astype(jnp.bfloat16)  287 us
    all_gather x1, waiting for transfers between devices, per_device(): lax.all_gather(own_rows, 'orb', axis=1, tiled=True)  107 us
    all_gather x1, waiting for transfers between devices, per_device(): lax.all_gather(point_rows, 'orb', axis=1, tiled=True)  51.5 us
    reduce_scatter x1, waiting for transfers between devices, per_device(): lax.psum_scatter(partial_matrix, 'grid', scatter_dimension=1, tiled=True)  43.8 us
    reduce_scatter x1, waiting for transfers between devices, per_device(): lax.psum_scatter(-lax.dot_general(applied, fitting, (((0,), (1,)), ((), (...  39.1 us
    gather x1, local copies, waits for them, and re-layouts, per_device(): taken = jnp.take(orbitals, clamped, axis=0).astype(jnp.float32)  34.9 us
    dot_general x1, matrix products, per_device(): jnp.dot(masked, point_full, preferred_element_type=jnp.float32)  27.6 us
  transfers between devices with their start and end apart: 6, of which 5 were waited for; matrix products, arithmetic and copies ran while one was open for 3% of the time, Pallas kernels for 0%

profile of v1, /device:TPU:0, one launch (start us, length us, event | category | flops | bytes accessed | tf_op | source)
XLA Modules:
  0.0 1214.7 jit_solution(13406106823982599792)
XLA Ops:
  7.2 0.0 copy-start
  7.2 0.0 all-gather.5.cloned.1.call-start
  7.2 0.8 compare_and_fusion.1
  8.1 0.8 fusion.11
  8.8 34.9 %gather_fusion = bf16[8192,512]{1,0:T(8,128)(2,1)} fusion(bf16[256,512]{1,0:T(8,128)(2,1)} %param.4, s32[8192]{0:T(1024)S(1)} %fusion.11), kind=kCustom, calls=%fused_computation | custom fusion | bytes 16809984 | tf_op jit(solution)/shard_map/jit(_take)/gather | solution.py:22
  43.7 8.6 select_convert_fusion
  52.3 0.0 all-gather.5.cloned.1.call-update
  52.3 0.0 all-gather.9.cloned.1.call-start
  52.4 564.2 %all-gather.5.cloned.1.call-done = bf16[4,8192,512]{2,1,0:T(8,128)(2,1)} async-done(((bf16[1,8192,512]{2,1,0:T(8,128)(2,1)}), bf16[4,8192,512]{2,1,0:T(8,128)(2,1)}) %all-gather.5.cloned.1.call-update) | async-done | bytes 33554448 | tf_op jit(solution)/shard_map/all_gather | solution.py:24
  616.6 16.3 %reduce_sum.12 = bf16[8192,512]{1,0:T(8,128)(2,1)} reduce(bf16[4,8192,512]{2,1,0:T(8,128)(2,1)} %all-gather.5.cloned.1.call-done, bf16[]{:T(256)} %constant.21.clone.1), dimensions={0}, to_apply=%region_0.1 | reduce | flops 12582912 | bytes 41943040 | tf_op jit(solution)/shard_map/reduce_sum | solution.py:24
  632.9 3.0 constant_dynamic-slice_fusion
  635.9 0.0 all-gather.9.cloned.1.call-update
  636.0 0.0 all-gather.7.cloned.1.call-start
  636.0 4.4 constant_dynamic-slice_fusion.1
  640.4 0.0 all-gather.7.cloned.1.call-update
  640.5 0.0 all-gather.11.cloned.1.call-start
  640.5 0.5 all-gather.11.cloned.1.call-update
  641.0 0.0 reduce-scatter.3.cloned.1.call-start
  641.1 51.5 %all-gather.9.cloned.1.call-done = bf16[2048,2048]{1,0:T(8,128)(2,1)} async-done(((bf16[2048,512]{1,0:T(8,128)(2,1)}), bf16[2048,2048]{1,0:T(8,128)(2,1)}) %all-gather.9.cloned.1.call-update) | async-done | bytes 8388624 | tf_op jit(solution)/shard_map/all_gather | solution.py:32
  692.6 107.5 %all-gather.7.cloned.1.call-done = bf16[4096,2048]{1,0:T(8,128)(2,1)} async-done(((bf16[4096,512]{1,0:T(8,128)(2,1)}), bf16[4096,2048]{1,0:T(8,128)(2,1)}) %all-gather.7.cloned.1.call-update) | async-done | bytes 16777232 | tf_op jit(solution)/shard_map/all_gather | solution.py:31
  800.1 27.6 %fusion.4 = f32[1024,2048]{1,0:T(8,128)} fusion(bf16[2048,2048]{1,0:T(8,128)(2,1)} %all-gather.9.cloned.1.call-done, bf16[1024,2048]{1,0:T(8,128)(2,1)} %param.7, bf16[4096,2048]{1,0:T(8,128)(2,1)} %all-gather.7.cloned.1.call-done, s32[]{:T(128)S(6)} %select_n.41), kind=kOutput, calls=%fused_computation.7 | convolution fusion | flops 17186160640 | bytes 33554436 | tf_op jit(solution)/shard_map/dot_general | solution.py:39
  827.7 287.3 %all-reduce.1 = bf16[1024,2048]{1,0:T(8,128)(2,1)} all-reduce(f32[1024,2048]{1,0:T(8,128)} %fusion.4), channel_id=1, replica_groups=mesh['grid'=4,'orb'=4,'pts'=2] {'grid'}, use_global_device_ids=true, to_apply=%region_1.2 | all-reduce | flops 2097152 | bytes 12582912 | tf_op jit(solution)/shard_map/psum | solution.py:40
  1115.0 0.0 copy-done
  1115.0 4.8 fusion.6
  1119.8 0.0 reduce-scatter.3.cloned.1.call-update
  1119.9 0.0 reduce-scatter.5.cloned.1.call-start
  1119.9 0.0 all-gather.11.cloned.1.call-done
  1119.9 39.1 %reduce-scatter.3.cloned.1.call-done = f32[256,256]{1,0:T(8,128)} async-done(((f32[2048,256]{1,0:T(8,128)}), f32[256,256]{1,0:T(8,128)}) %reduce-scatter.3.cloned.1.call-update) | async-done | bytes 262160 | tf_op jit(solution)/shard_map/reduce_scatter | solution.py:41
  1159.1 3.1 fusion.9
  1162.1 0.0 reduce-scatter.5.cloned.1.call-update
  1162.2 43.8 %reduce-scatter.5.cloned.1.call-done = f32[256,512]{1,0:T(8,128)} async-done(((f32[256,2048]{1,0:T(8,128)}), f32[256,512]{1,0:T(8,128)}) %reduce-scatter.5.cloned.1.call-update) | async-done | bytes 524304 | tf_op jit(solution)/shard_map/reduce_scatter | solution.py:55
  1206.0 1.9 broadcast_multiply_fusion
Async XLA Ops:
  7.2 1107.8 %copy-start = (bf16[256,1024]{1,0:T(8,128)(2,1)S(1)}, bf16[256,1024]{1,0:T(8,128)(2,1)}, u32[]{:S(2)}) copy-start(bf16[256,1024]{1,0:T(8,128)(2,1)} %param.6) | copy-start | bytes 1572868
  7.2 609.4 %all-gather.5.cloned.1.call-start = ((), (), s32[]{:S(2)}) async-start(), calls=%async_computation.2 | async-start | bytes 41943040 | tf_op jit(solution)/shard_map/all_gather | solution.py:24
  52.3 640.2 %all-gather.9.cloned.1.call-start = ((), (), s32[]{:S(2)}) async-start(), calls=%async_computation.4 | async-start | bytes 10485760 | tf_op jit(solution)/shard_map/all_gather | solution.py:32
  636.0 164.1 %all-gather.7.cloned.1.call-start = ((), (), s32[]{:S(2)}) async-start(), calls=%async_computation.3 | async-start | bytes 20971520 | tf_op jit(solution)/shard_map/all_gather | solution.py:31
  640.5 479.5 %all-gather.11.cloned.1.call-start = ((), (), s32[]{:S(2)}) async-start(), calls=%async_computation.6 | async-start | bytes 1310720 | tf_op jit(solution)/shard_map/all_gather | solution.py:52
  641.0 518.0 %reduce-scatter.3.cloned.1.call-start = ((), (), s32[]{:S(2)}) async-start(), calls=%async_computation.5 | async-start | bytes 2359296 | tf_op jit(solution)/shard_map/reduce_scatter | solution.py:41
  1119.9 86.1 %reduce-scatter.5.cloned.1.call-start = ((), (), s32[]{:S(2)}) async-start(), calls=%async_computation.7 | async-start | bytes 2621440 | tf_op jit(solution)/shard_map/reduce_scatter | solution.py:55
Sparse Core Ops, SparseCore 0:
  52.4 564.0 all-gather.4
  636.1 56.4 all-gather.8
  694.1 105.8 all-gather.6
  801.5 16.6 all-gather.10
  1120.0 39.0 reduce-scatter.2
  1162.3 43.6 reduce-scatter.4
